TPU v7x, 32 devices: a whole 2x2x4 slice. The times are simulated.
32 devices in a mesh: grp: 8 (over y, x, core), sub: 4 (over z).
Axes of the slice: x: 2, y: 2, z: 4, core: 2. Of those that a mesh axis runs over, the one named last changes fastest.
Arguments:
- blocks: bfloat16 [256, 128, 128], P(('grp', 'sub')), may hold values from -0.5 to 0.5
- block_cols: int32 [256], P(('grp', 'sub')), may hold values from 0 to 31, as said below
- far_slots: int32 [32, 32], P(('grp', 'sub')), may hold values from 0 to 7, as said below
- pair_lists: int32 [32, 4, 128], P(('grp', 'sub')), may hold values from 0 to 7, as said below
Outputs:
- participation: float32 [4096], P(('grp', 'sub'))
- total: float32 [], replicated
Inputs may be any that keep to these rules, and one draw needn't show every extreme that they name: `block_cols`: the block column of slot t is at most its block row t // 8. `far_slots`: the 4 slots of one block row and source group are distinct. `pair_lists`: rows 0 and 2 hold slot numbers below 8, row 1 positions below 4, row 3 holds 0 or 1; within one block row and source group no two triples share both their left slot and far position.
All inputs are finite; a program needn't handle non-finite values.
Results may differ from a plain program's by a relative error of at most 0.00035.
Values may be sent and summed in bfloat16 or wider, within the bound.
No kernel may reach another device: no remote copies, remote signals or barrier semaphores. Data moves between devices by JAX's collectives and lax.ppermute only.
A program may use at most 64 MiB of HBM per device.

v0:
```python
import math

import jax
import jax.numpy as jnp
from jax import lax
from jax.sharding import PartitionSpec as P


def select_rows(indices, table):
    choices_of = (indices[:, None] == jnp.arange(table.shape[0], dtype=jnp.int32)[None, :]).astype(
        table.dtype
    )
    return jnp.dot(choices_of, table, preferred_element_type=jnp.float32).astype(table.dtype)


def triple_sums(left, far, mask, live, size):
    count = left.shape[0]
    left_blocks = left.reshape(count, size, size)
    far_blocks = far.reshape(count, size, size)
    mask_blocks = mask.reshape(count, size, size)
    product = jnp.einsum(
        "wik,wkj->wij", left_blocks, far_blocks, preferred_element_type=jnp.float32
    )
    sums = jnp.sum(mask_blocks.astype(jnp.float32) * product, axis=2)
    return jnp.dot(live.astype(jnp.float32), sums, precision=lax.Precision.HIGHEST)


def local(blocks, block_cols, far_slots, pair_lists):
    stored = blocks.shape[0]
    size = blocks.shape[1]
    groups = lax.axis_size("grp")
    subs = lax.axis_size("sub")
    myself = lax.axis_index(("grp", "sub"))
    inner = jnp.arange(size, dtype=jnp.int32)
    strict = inner[:, None] > inner[None, :]
    on_diag = block_cols == myself
    own = jnp.where(
        on_diag[:, None, None] & jnp.logical_not(strict)[None], jnp.zeros((), blocks.dtype), blocks
    )
    own_flat = own.reshape(stored, size * size)
    lists = pair_lists[0]
    per_source = lists.shape[1] // groups
    left_idx = lists[0].reshape(groups, per_source)
    far_idx = lists[1].reshape(groups, per_source)
    mask_idx = lists[2].reshape(groups, per_source)
    live_idx = lists[3].reshape(groups, per_source)
    wanted_row = far_slots[0].reshape(groups, far_slots.shape[1] // groups)
    requests = lax.all_to_all(wanted_row, "grp", split_axis=0, concat_axis=0, tiled=True)
    outgoing = jax.vmap(lambda wanted: select_rows(wanted, own_flat))(requests)
    fetched = lax.all_to_all(outgoing, "grp", split_axis=0, concat_axis=0, tiled=True)

    def one_source(running, item):
        chosen, left_slot, far_place, mask_slot, live = item
        far = select_rows(far_place, chosen)
        left = select_rows(left_slot, own_flat)
        mask = select_rows(mask_slot, own_flat)
        return (running + triple_sums(left, far, mask, live, size), None)

    participation, unused = lax.scan(
        one_source,
        jnp.zeros((size,), jnp.float32),
        (fetched, left_idx, far_idx, mask_idx, live_idx),
    )
    summed = lax.psum(jnp.sum(participation), ("grp", "sub"))
    total = summed / math.sqrt(groups * subs * size)
    return (participation, total)


def solution(mesh):
    placed = (
        P(("grp", "sub"), None, None),
        P(("grp", "sub")),
        P(("grp", "sub"), None),
        P(("grp", "sub"), None, None),
    )
    return jax.shard_map(
        local, mesh=mesh, in_specs=placed, out_specs=(P(("grp", "sub")), P()), check_vma=False
    )
```

profile of v0, /device:TPU:0, one launch (start us, length us, event | category | flops | bytes accessed | tf_op | source)
XLA Modules:
  0.0 96.6 jit_solution(1881355058255295593)
XLA Ops:
  0.6 0.5 broadcast.29
  1.1 1.3 %reduce.19 = s32[32]{0:T(128)S(1)} reduce(s32[1,32]{1,0:T(1,128)} %param.8, s32[]{:T(128)} %broadcast.29), dimensions={0}, to_apply=%param.8.reduce_sub_computation.3 | reduce | bytes 260 | tf_op args[2]
  2.5 0.7 all_to_all.9
  3.1 5.2 %all-to-all-start = ((s32[8,1,4]{2,1,0:T(1,128)}), s32[8,1,4]{2,1,0:T(1,128)S(1)}, u32[]{:S(2)}, u32[]{:S(2)}) async-start(s32[8,1,4]{2,1,0:T(1,128)} %bitcast), calls=%async_computation | async-start | bytes 8192 | tf_op jit(solution)/shard_map/all_to_all | solution.py:48
  8.4 0.7 broadcast_compare_fusion
  9.0 1.1 %and_select_fusion = bf16[8,128,128]{2,1,0:T(8,128)(2,1)S(1)} fusion(bf16[8,128,128]{2,1,0:T(8,128)(2,1)} %param.6, pred[128,128]{1,0:T(8,128)(4,1)S(1)} %fusion.18, pred[8]{0:T(512)(128)(4,1)S(1)} %broadcast_compare_fusion), kind=kLoop, calls=%fused_computation.31 | loop fusion | flops 262144 | bytes 540680 | tf_op jit(solution)/shard_map/jit(_where)/select_n | solution.py:37
  10.3 2.8 %all-to-all-done = s32[8,1,4]{2,1,0:T(1,128)S(1)} async-done(((s32[8,1,4]{2,1,0:T(1,128)}), s32[8,1,4]{2,1,0:T(1,128)S(1)}, u32[]{:S(2)}, u32[]{:S(2)}) %all-to-all-start) | async-done | bytes 160 | tf_op jit(solution)/shard_map/all_to_all | solution.py:48
  13.1 0.5 convolution_convert_fusion.3
  13.6 1.8 %copy.14 = bf16[8,4,16384]{2,1,0:T(4,128)(2,1)} copy(bf16[8,4,16384]{2,0,1:T(8,128)(2,1)S(1)} %convolution_convert_fusion.3) | data formatting | bytes 2097152 | tf_op jit(solution)/shard_map/vmap()/convert_element_type | solution.py:13
  15.4 3.7 %all-to-all-start.1 = ((bf16[8,4,16384]{2,1,0:T(4,128)(2,1)}), bf16[8,4,16384]{2,1,0:T(4,128)(2,1)S(1)}, u32[]{:S(2)}, u32[]{:S(2)}) async-start(bf16[8,4,16384]{2,1,0:T(4,128)(2,1)} %copy.14), calls=%async_computation.1 | async-start | bytes 2097152 | tf_op jit(solution)/shard_map/all_to_all | solution.py:50
  19.3 0.2 fusion.26
  19.5 0.2 copy.21
  19.8 14.6 %all-to-all-done.1 = bf16[8,4,16384]{2,1,0:T(4,128)(2,1)S(1)} async-done(((bf16[8,4,16384]{2,1,0:T(4,128)(2,1)}), bf16[8,4,16384]{2,1,0:T(4,128)(2,1)S(1)}, u32[]{:S(2)}, u32[]{:S(2)}) %all-to-all-start.1) | async-done | bytes 1048608 | tf_op jit(solution)/shard_map/all_to_all | solution.py:50
  34.4 20.1 %while.11 = (s32[]{:T(128)}, f32[128]{0:T(128)S(1)}, s32[8,16]{1,0:T(8,128)S(1)}, s32[8,16]{1,0:T(8,128)S(1)}, bf16[8,16384]{1,0:T(8,128)(2,1)S(1)}, /*index=5*/...) while((s32[]{:T(128)}, f32[128]{0:T(128)S(1)}, ...), condition=%wide.region_2.3_spmd.clone, body=%wide.region_0.2_spmd.clone.sunk | while | flops 79190608 | bytes 11160199 | solution.py:59
  34.4 0.3 fusion.49
  34.8 0.2 copy.26
  35.0 0.3 copy.27
  35.3 0.3 fusion.50
  35.8 0.3 fusion.52
  36.2 0.5 fusion.53
  36.9 0.4 fusion.49
  37.3 0.2 copy.26
  37.5 0.3 copy.27
  37.8 0.3 fusion.50
  38.3 0.3 fusion.52
  38.7 0.5 fusion.53
  39.4 0.4 fusion.49
  39.8 0.2 copy.26
  40.0 0.3 copy.27
  40.3 0.3 fusion.50
  40.8 0.3 fusion.52
  41.3 0.5 fusion.53
  41.9 0.4 fusion.49
  42.3 0.2 copy.26
  42.5 0.3 copy.27
  42.9 0.3 fusion.50
  43.3 0.3 fusion.52
  43.8 0.5 fusion.53
  44.5 0.4 fusion.49
  44.8 0.2 copy.26
  45.0 0.3 copy.27
  45.4 0.3 fusion.50
  45.8 0.3 fusion.52
  46.3 0.5 fusion.53
  47.0 0.4 fusion.49
  47.3 0.2 copy.26
  47.6 0.3 copy.27
  47.9 0.3 fusion.50
  48.4 0.3 fusion.52
  48.8 0.5 fusion.53
  49.5 0.4 fusion.49
  49.9 0.2 copy.26
  50.1 0.3 copy.27
  50.4 0.3 fusion.50
  50.9 0.3 fusion.52
  51.3 0.5 fusion.53
  52.0 0.4 fusion.49
  52.4 0.2 copy.26
  52.6 0.3 copy.27
  52.9 0.3 fusion.50
  53.4 0.3 fusion.52
  53.8 0.5 fusion.53
  54.5 0.6 reduce_sum.18
  55.1 39.7 %psum.7 = f32[]{:T(128)} all-reduce(f32[]{:T(128)} %reduce_sum.18), channel_id=1, replica_groups=mesh['grp'=8,'sub'=4] {'grp','sub'}, use_global_device_ids=true, to_apply=%region_4.5 | all-reduce | flops 1 | bytes 8 | tf_op jit(solution)/shard_map/psum | solution.py:64
  (55 shorter events, 3.3 us)
Async XLA Ops:
  3.1 9.9 %all-to-all-start = ((s32[8,1,4]{2,1,0:T(1,128)}), s32[8,1,4]{2,1,0:T(1,128)S(1)}, u32[]{:S(2)}, u32[]{:S(2)}) async-start(s32[8,1,4]{2,1,0:T(1,128)} %bitcast), calls=%async_computation | async-start | bytes 8192 | tf_op jit(solution)/shard_map/all_to_all | solution.py:48
  15.4 3.7 %copy-start.2 = (s32[1,4,128]{2,1,0:T(4,128)S(1)}, s32[1,4,128]{2,1,0:T(4,128)}, u32[]{:S(2)}) copy-start(s32[1,4,128]{2,1,0:T(4,128)} %param.9) | copy-start | bytes 6148
  15.4 3.9 %copy-start = (bf16[8,128,128]{2,1,0:T(8,128)(2,1)S(1)}, bf16[8,128,128]{2,1,0:T(8,128)(2,1)}, u32[]{:S(2)}) copy-start(bf16[8,128,128]{2,1,0:T(8,128)(2,1)} %param.6) | copy-start | bytes 786436
  15.4 19.0 %all-to-all-start.1 = ((bf16[8,4,16384]{2,1,0:T(4,128)(2,1)}), bf16[8,4,16384]{2,1,0:T(4,128)(2,1)S(1)}, u32[]{:S(2)}, u32[]{:S(2)}) async-start(bf16[8,4,16384]{2,1,0:T(4,128)(2,1)} %copy.14), calls=%async_computation.1 | async-start | bytes 2097152 | tf_op jit(solution)/shard_map/all_to_all | solution.py:50
  54.5 41.0 %copy-start.1 = (f32[128]{0:T(128)}, f32[128]{0:T(128)S(1)}, u32[]{:S(2)}) copy-start(f32[128]{0:T(128)S(1)} %get-tuple-element.42) | copy-start | bytes 1540
where the time goes:
time: 97.1 us; the launch traced here: 96.6 us
  blocking collectives  39.7 us (41%)
  waiting for transfers between devices  17.4 us (18%)
  matrix products  14.2 us (15%)
  local copies, waits for them, and re-layouts  9.57 us (10%)
  starting transfers between devices  8.89 us (9%)
  other arithmetic  3.88 us (4%)
  between operations  2.49 us (3%)
    psum x1, blocking collectives, local(): summed = lax.psum(jnp.sum(participation), ('grp', 'sub'))  39.7 us
    all_to_all x1, waiting for transfers between devices, local(): lax.all_to_all(outgoing, 'grp', split_axis=0, concat_axis=0, tiled=True)  14.6 us
    dot_general x25, matrix products, select_rows(): jnp.dot(choices_of, table, preferred_element_type=jnp.float32)  8.81 us
    all_to_all x1, starting transfers between devices, local(): lax.all_to_all(wanted_row, 'grp', split_axis=0, concat_axis=0, tiled=True)  5.2 us
    dot_general x8, matrix products, triple_sums(): jnp.einsum('wik,wkj->wij', left_blocks, far_blocks, preferred_element_typ...  4.22 us
    all_to_all x1, starting transfers between devices, local(): lax.all_to_all(outgoing, 'grp', split_axis=0, concat_axis=0, tiled=True)  3.69 us
    while x24, local copies, waits for them, and re-layouts  3.1 us
    all_to_all x1, waiting for transfers between devices, local(): lax.all_to_all(wanted_row, 'grp', split_axis=0, concat_axis=0, tiled=True)  2.76 us
  transfers between devices with their start and end apart: 2, of which 2 were waited for; matrix products, arithmetic and copies ran while one was open for 3% of the time, Pallas kernels for 0%

commit v1 on v0

v1 whole, which is shorter than its diff:
```python
import functools
import itertools
import math

import jax
import jax.numpy as jnp
from jax import lax
from jax.experimental import pallas as pl
from jax.experimental.pallas import tpu as pltpu
from jax.sharding import PartitionSpec as P

FIELD = 8


class Places:
    def __init__(self, count):
        self.count = count
        self.cycle = 4 if count % 4 == 0 else count
        self.mids = count // self.cycle

    def split(self, place):
        if self.cycle != 4:
            return (place, 0)
        low = place % 2
        high = place // (2 * self.mids)
        turn = 2 * low + high * (3 - 4 * low)
        return (turn, (place // 2) % self.mids)

    def join(self, turn, mid):
        if self.cycle != 4:
            return turn
        return (turn % 2) * 2 * self.mids + mid * 2 + ((turn + 1) // 2) % 2

    def step(self, place, by):
        turn, mid = self.split(place)
        return self.join((turn + by[0]) % self.cycle, (mid + by[1]) % self.mids)

    def gap(self, there, here):
        return ((there[0] - here[0]) % self.cycle, (there[1] - here[1]) % self.mids)

    def cover(self):
        steps = sorted(
            itertools.product(range(self.cycle), range(self.mids)),
            key=lambda s: ((s[0] > 0) + (s[1] > 0), s),
        )

        def reached(chosen):
            return {self.gap(a, b) for a in chosen for b in chosen}

        chosen = [(0, 0)]
        while len(reached(chosen)) < self.count:
            chosen.append(max(steps, key=lambda s: len(reached(chosen + [s]))))
        held = sorted(chosen, key=lambda s: (s != (0, 0), s != (2, 0), s))
        pairs = {}
        for (i, row), (j, source) in itertools.product(enumerate(held), enumerate(held)):
            wanted = self.gap(source, row)
            if wanted not in pairs or max(i, j) < max(pairs[wanted]):
                pairs[wanted] = (i, j)
        return held, sorted(pairs.values())


class Plan:
    def __init__(self, groups, subs, width, far_width):
        self.groups = groups
        self.subs = subs
        self.listed = width // groups
        self.named = far_width // groups
        self.places = Places(groups)
        self.held, self.pairs = self.places.cover()
        self.near = 2 if (2, 0) in self.held and len(self.held) > 2 else 1
        self.order = sorted(range(len(self.held)), key=lambda i: (self.held[i] == (2, 0), i))

    def group(self, i):
        return self.places.step(lax.axis_index("grp"), self.held[i])

    def owner(self, i):
        return self.group(i) * self.subs + lax.axis_index("sub")


def pack_kernel(plan, pair_lists, far_slots, block_cols, raw, meta, strict, kept):
    groups, listed, named = plan.groups, plan.listed, plan.named
    stored, size = raw.shape[:2]
    left, place, mask, live = (pair_lists[0, field : field + 1] for field in range(4))
    width = place.shape[1]
    spread = lax.broadcasted_iota(jnp.int32, (groups * named, width), 0)
    source = lax.broadcasted_iota(jnp.int32, (groups * named, width), 1) // listed
    wanted = (spread == source * named + place).astype(jnp.float32)
    slots = jnp.broadcast_to(far_slots[...].astype(jnp.float32), (8, groups * named))
    far = jnp.dot(slots, wanted, preferred_element_type=jnp.float32)[:1].astype(jnp.int32)
    codes = left + far * 2**FIELD + jnp.where(live == 1, mask, stored) * 4**FIELD
    for group in range(groups):
        meta[group, :, :listed] = codes[:, group * listed : (group + 1) * listed]
    for slot in range(stored):
        meta[groups + slot] = jnp.full((1, size), block_cols[slot] != plan.owner(0), meta.dtype)
    rows = lax.broadcasted_iota(jnp.int32, (size, size), 0)
    columns = lax.broadcasted_iota(jnp.int32, (size, size), 1)
    strict[...] = (rows > columns).astype(jnp.float32).astype(strict.dtype)
    keep_strict(groups, raw, meta, strict, kept)


def keep_strict(groups, raw, meta, strict, kept, wide=None):
    stored = raw.shape[0]
    for slot in range(stored):
        off_diag = meta[groups + slot].astype(jnp.float32).astype(kept.dtype)
        kept[slot] = raw[slot] * jnp.maximum(strict[...], off_diag)
        if wide is not None:
            wide[slot] = kept[slot].astype(wide.dtype)
    kept[stored] = jnp.zeros_like(kept[stored])
    if wide is not None:
        wide[stored] = jnp.zeros_like(wide[stored])


def add_triples(plan, acc, row, masks, source, codes):
    field = 2**FIELD - 1
    for w in range(plan.listed):
        code = codes[0, w]
        left = row[code & field]
        far = source[(code >> FIELD) & field]
        mask = masks[code >> (2 * FIELD)]
        acc = acc + mask.astype(jnp.float32) * jnp.dot(left, far, preferred_element_type=jnp.float32)
    return acc


def stage_kernel(plan, first, last, new, pairs, *refs):
    refs = list(refs)
    strict = refs.pop(0)
    metas = [refs.pop(0) for _ in range(new.stop)]
    kept = [refs.pop(0) for _ in range(new.start)]
    raws = [refs.pop(0) for _ in new]
    before = None if first else refs.pop(0)
    if not last:
        kept += [refs.pop(0) for _ in new]
    out = refs.pop(0)
    if last:
        kept += [refs.pop(0) for _ in new]

    for i in new:
        keep_strict(plan.groups, raws[i - new.start], metas[i], strict, kept[i])
    size = kept[0].shape[1]
    done = 0 if first else new.start
    sums = {}
    for i in range(new.stop):
        acc = before[i] if i < done else jnp.zeros((size, size), jnp.float32)
        for row, j in pairs:
            if row == i:
                acc = add_triples(plan, acc, kept[i], kept[i], kept[j], metas[i][plan.group(j)])
        if last:
            sums[i] = jnp.sum(acc.T, axis=0, keepdims=True)
        else:
            out[i] = acc
    if not last:
        return
    out[:, :, :size] = jnp.zeros((out.shape[0], 1, size), out.dtype)
    out[:, :, size:] = jnp.broadcast_to(sum(sums.values())[None], (out.shape[0], 1, size))
    for i, vector in sums.items():
        out[plan.owner(i), :, :size] = vector


def last_kernel(divisor, received, participation, total):
    size = participation.shape[0]
    summed = jnp.sum(received[:, 0, :], axis=0, keepdims=True)
    participation[...] = summed[0, :size]
    total[0] = jnp.sum(summed[:, size:]) / divisor


def in_vmem(array):
    return pltpu.with_memory_space_constraint(array, pltpu.VMEM)


def local(blocks, block_cols, far_slots, pair_lists):
    stored, size = blocks.shape[:2]
    groups = lax.axis_size("grp")
    subs = lax.axis_size("sub")
    width = pair_lists.shape[2]
    far_width = far_slots.shape[1]
    plan = Plan(groups, subs, width, far_width)
    held = plan.held

    def brought(array, i):
        if i == 0:
            return array
        pairs = [(plan.places.step(g, held[i]), g) for g in range(groups)]
        return lax.ppermute(array, "grp", pairs)

    raws = {i: brought(blocks, i) for i in plan.order}
    kept_shape = (stored + 1, size, size)
    own_vmem = pltpu.CompilerParams(vmem_limit_bytes=16 * 2**20)
    smem = pl.BlockSpec(memory_space=pltpu.SMEM)
    vmem = pl.BlockSpec(memory_space=pltpu.VMEM)
    meta, strict, own = pl.pallas_call(
        functools.partial(pack_kernel, plan),
        out_shape=[
            pltpu.VMEM((groups + stored, 1, size), jnp.int32),
            pltpu.VMEM((size, size), blocks.dtype),
            pltpu.VMEM(kept_shape, blocks.dtype),
        ],
        in_specs=[vmem, vmem, smem, vmem],
        out_specs=[vmem, vmem, vmem],
        compiler_params=own_vmem,
        name="pack",
    )(pair_lists, far_slots, block_cols, blocks)
    metas = {i: brought(meta, i) for i in plan.order}

    stages = [range(1, plan.near)] + [range(i, i + 1) for i in range(plan.near, len(held))]
    kept = [own]
    sums = []
    for at, new in enumerate(stages):
        first, last = at == 0, at == len(stages) - 1
        pairs = [p for p in plan.pairs if max(p) in new or first and max(p) == 0]
        if last:
            out_shape = pltpu.VMEM((groups * subs, 1, 2 * size), jnp.float32)
        else:
            out_shape = [pltpu.VMEM(kept_shape, blocks.dtype)] * len(new)
            out_shape += [pltpu.VMEM((new.stop, size, size), jnp.float32)]
        operands = [in_vmem(a) for a in [strict] + [metas[i] for i in range(new.stop)] + kept + [raws[i] for i in new] + sums]
        call = pl.pallas_call(
            functools.partial(stage_kernel, plan, first, last, new, pairs),
            out_shape=out_shape,
            in_specs=[vmem] * len(operands),
            out_specs=vmem if last else [vmem] * (len(new) + 1),
            scratch_shapes=[pltpu.VMEM(kept_shape, blocks.dtype)] * len(new) if last else [],
            cost_estimate=pl.CostEstimate(
                flops=len(pairs) * plan.listed * 2 * size**3,
                bytes_accessed=2 * len(new) * stored * size * size * blocks.dtype.itemsize,
                transcendentals=0,
            ),
            compiler_params=own_vmem,
        )
        out = call(*operands)
        if not last:
            kept += out[:-1]
            sums = [out[-1]]
    received = in_vmem(lax.all_to_all(out, ("grp", "sub"), split_axis=0, concat_axis=0, tiled=True))
    participation, total = pl.pallas_call(
        functools.partial(last_kernel, math.sqrt(groups * subs * size)),
        out_shape=[jax.ShapeDtypeStruct((size,), jnp.float32), jax.ShapeDtypeStruct((1,), jnp.float32)],
        in_specs=[vmem],
        out_specs=[vmem, smem],
        compiler_params=own_vmem,
        name="last",
    )(received)
    return (participation, total[0])


def solution(mesh):
    placed = (
        P(("grp", "sub"), None, None),
        P(("grp", "sub")),
        P(("grp", "sub"), None),
        P(("grp", "sub"), None, None),
    )

    return jax.shard_map(local, mesh=mesh, in_specs=placed, out_specs=(P(("grp", "sub")), P()), check_vma=False)
```

time: 97.1 us -> 27.2 us (0.28)
  blocking collectives: 39.7 us -> 11.9 us
  waiting for transfers between devices: 17.4 us -> 2.2 us
  matrix products: 14.2 us -> 0 us
  local copies, waits for them, and re-layouts: 9.57 us -> 2.97 us
  other arithmetic: 3.88 us -> 0 us
  Pallas kernels: 0 us -> 3.72 us
  starting transfers between devices: 8.89 us -> 5.52 us
  between operations: 2.49 us -> 0.68 us
    psum x1 -> x0, blocking collectives: 39.7 us -> none  [local(): summed = lax.psum(jnp.sum(participation), ('grp', 'sub'))]
    all_to_all x2 -> x0, waiting for transfers between devices: 17.4 us -> none  [the longest x1 14.6 us: local(): lax.all_to_all(outgoing, 'grp', split_axis=0, concat_axis=0, tiled=True)]
    dot_general x41 -> x0, matrix products: 14.2 us -> none  [the longest x25 8.81 us: select_rows(): jnp.dot(choices_of, table, preferred_element_type=jnp.float32)]
    all_to_all x0 -> x1, blocking collectives: none -> 11.9 us  [local(): lax.all_to_all(out, ('grp', 'sub'), split_axis=0, concat_axis=0, tiled=True)]
    all_to_all x2 -> x0, starting transfers between devices: 8.89 us -> none  [the longest x1 5.2 us: local(): lax.all_to_all(wanted_row, 'grp', split_axis=0, concat_axis=0, tiled=True)]
    ppermute x0 -> x6, starting transfers between devices: none -> 5.52 us  [brought(): return lax.ppermute(array, 'grp', pairs)]
    convert_element_type x9 -> x0, local copies, waits for them, and re-layouts: 4.45 us -> none  [the longest x8 2.65 us: triple_sums(): sums = jnp.sum(mask_blocks.astype(jnp.float32) * product, axis=2)]
    pallas_call x0 -> x5, Pallas kernels: none -> 3.72 us  [the longest x3 2.33 us: local(): out = call(*operands)]
  transfers between devices with their start and end apart: 2 -> 6, of which waited for: 2 -> 2; matrix products, arithmetic and copies ran while one was open for 3% -> 0% of each run, Pallas kernels for 0% -> 7%
where the time goes in v1:
time: 27.2 us; the launch traced here: 27 us
  blocking collectives  11.9 us (44%)
  starting transfers between devices  5.52 us (20%)
  Pallas kernels  3.72 us (14%)
  local copies, waits for them, and re-layouts  2.97 us (11%)
  waiting for transfers between devices  2.2 us (8%)
  between operations  0.68 us (2%)
    all_to_all x1, blocking collectives, local(): lax.all_to_all(out, ('grp', 'sub'), split_axis=0, concat_axis=0, tiled=True)  11.9 us
    ppermute x6, starting transfers between devices, brought(): return lax.ppermute(array, 'grp', pairs)  5.52 us
    unnamed x8, local copies, waits for them, and re-layouts  2.97 us
    pallas_call x3, Pallas kernels, local(): out = call(*operands)  2.33 us
    ppermute x6, waiting for transfers between devices, brought(): return lax.ppermute(array, 'grp', pairs)  2.2 us
    pallas_call x1, Pallas kernels, local(): pl.pallas_call(functools.partial(pack_kernel, plan), out_shape=[pltpu.VME...  0.74 us
    pallas_call x1, Pallas kernels, local(): pl.pallas_call(functools.partial(last_kernel, math.sqrt(groups * subs * s...  0.66 us
  transfers between devices with their start and end apart: 6, of which 2 were waited for; matrix products, arithmetic and copies ran while one was open for 0% of the time, Pallas kernels for 7%

profile of v1, /device:TPU:0, one launch (start us, length us, event | category | flops | bytes accessed | tf_op | source)
XLA Modules:
  0.0 27.0 jit_solution(11680100505475082811)
XLA Ops:
  0.6 0.6 %collective-permute-start.3 = (bf16[8,128,128]{2,1,0:T(8,128)(2,1)}, bf16[8,128,128]{2,1,0:T(8,128)(2,1)S(1)}, u32[]{:S(2)}, u32[]{:S(2)}) collective-permute-start(bf16[8,128,128]{2,1,0:T(8,128)(2,1)} %raw.1), channel_id=1, source_target_pairs={{4,0},{0,4},{12,8},{8,12},{20,16},{16,20},{28,24},{24,28},{5,1},{1... | collective-permute-start | bytes 786440 | tf_op jit(solution)/shard_map/ppermute | solution.py:183
  1.2 2.6 %collective-permute-start.4 = (bf16[8,128,128]{2,1,0:T(8,128)(2,1)}, bf16[8,128,128]{2,1,0:T(8,128)(2,1)S(1)}, u32[]{:S(2)}, u32[]{:S(2)}) collective-permute-start(bf16[8,128,128]{2,1,0:T(8,128)(2,1)} %raw.1), channel_id=1, source_target_pairs={{8,0},{12,4},{0,8},{4,12},{24,16},{28,20},{16,24},{20,28},{9,1},{1... | collective-permute-start | bytes 786440 | tf_op jit(solution)/shard_map/ppermute | solution.py:183
  3.7 1.5 %collective-permute-start.5 = (bf16[8,128,128]{2,1,0:T(8,128)(2,1)}, bf16[8,128,128]{2,1,0:T(8,128)(2,1)S(1)}, u32[]{:S(2)}, u32[]{:S(2)}) collective-permute-start(bf16[8,128,128]{2,1,0:T(8,128)(2,1)} %raw.1), channel_id=1, source_target_pairs={{20,0},{16,4},{28,8},{24,12},{0,16},{4,20},{8,24},{12,28},{21,1},{... | collective-permute-start | bytes 786440 | tf_op jit(solution)/shard_map/ppermute | solution.py:183
  5.3 0.0 copy-start
  5.3 1.0 %copy-done = bf16[8,128,128]{2,1,0:T(8,128)(2,1)S(1)} copy-done((bf16[8,128,128]{2,1,0:T(8,128)(2,1)S(1)}, bf16[8,128,128]{2,1,0:T(8,128)(2,1)}, u32[]{:S(2)}) %copy-start) | copy-done | bytes 262168
  6.2 0.0 copy-start.1
  6.2 0.7 %copy-done.1 = s32[1,4,128]{2,1,0:T(4,128)S(1)} copy-done((s32[1,4,128]{2,1,0:T(4,128)S(1)}, s32[1,4,128]{2,1,0:T(4,128)}, u32[]{:S(2)}) %copy-start.1) | copy-done | bytes 2072
  6.9 0.0 copy-start.2
  6.9 0.7 %copy-done.2 = s32[1,32]{1,0:T(1,128)S(1)} copy-done((s32[1,32]{1,0:T(1,128)S(1)}, s32[1,32]{1,0:T(1,128)}, u32[]{:S(2)}) %copy-start.2) | copy-done | bytes 152
  7.6 0.0 copy-start.3
  7.6 0.7 %copy-done.3 = s32[8]{0:T(128)S(1)} copy-done((s32[8]{0:T(128)S(1)}, s32[8]{0:T(128)}, u32[]{:S(2)}) %copy-start.3) | copy-done | bytes 56
  8.2 0.7 %pack.1 = (s32[16,1,128]{2,1,0:T(1,128)S(1)}, bf16[128,128]{1,0:T(8,128)(2,1)S(1)}, bf16[9,128,128]{2,1,0:T(8,128)(2,1)S(1)}) custom-call(s32[1,4,128]{2,1,0:T(4,128)S(1)} %copy-done.1, s32[1,32]{1,0:T(1,128)S(1)} %copy-done.2, s32[8]{0:T(128)S(1)} %copy-done.3, bf16[8,128,128]{2,1,0:T(8,128)(2,1)S(1)} %copy-done), custom_call_target="tpu_custom_call" | custom-call | tf_op jit(solution)/shard_map/pack/pallas_call | solution.py:190
  9.0 0.0 collective-permute-start
  9.0 0.6 %collective-permute-start.1 = (s32[16,1,128]{2,1,0:T(1,128)S(1)}, s32[16,1,128]{2,1,0:T(1,128)S(1)}, u32[]{:S(2)}, u32[]{:S(2)}) collective-permute-start(s32[16,1,128]{2,1,0:T(1,128)S(1)} %get-tuple-element.12.refs_1_), channel_id=1, source_target_pairs={{8,0},{12,4},{0,8},{4,12},{24,16},{28,20},{16,24},{20,28},{9,1},{1... | collective-permute-start | bytes 24584 | tf_op jit(solution)/shard_map/ppermute | solution.py:183
  9.6 0.6 %collective-permute-done.refs_2_ = s32[16,1,128]{2,1,0:T(1,128)S(1)} collective-permute-done((s32[16,1,128]{2,1,0:T(1,128)S(1)}, s32[16,1,128]{2,1,0:T(1,128)S(1)}, u32[]{:S(2)}, u32[]{:S(2)}) %collective-permute-start) | collective-permute-done | bytes 8224 | tf_op jit(solution)/shard_map/ppermute | solution.py:183
  10.2 0.3 %collective-permute-start.2 = (s32[16,1,128]{2,1,0:T(1,128)S(1)}, s32[16,1,128]{2,1,0:T(1,128)S(1)}, u32[]{:S(2)}, u32[]{:S(2)}) collective-permute-start(s32[16,1,128]{2,1,0:T(1,128)S(1)} %get-tuple-element.12.refs_1_), channel_id=1, source_target_pairs={{20,0},{16,4},{28,8},{24,12},{0,16},{4,20},{8,24},{12,28},{21,1},{... | collective-permute-start | bytes 24584 | tf_op jit(solution)/shard_map/ppermute | solution.py:183
  10.4 0.0 collective-permute-done.3.refs_4_
  10.4 0.6 %shard_map.59 = (bf16[9,128,128]{2,1,0:T(8,128)(2,1)S(1)}, f32[2,128,128]{2,1,0:T(8,128)S(1)}) custom-call(bf16[128,128]{1,0:T(8,128)(2,1)S(1)} %get-tuple-element.11.refs_0_, s32[16,1,128]{2,1,0:T(1,128)S(1)} %get-tuple-element.12.refs_1_, s32[16,1,128]{2,1,0:T(1,128)S(1)} %collective-permute-done.refs_2_, ...), custom_call_target="tpu_custom_call" | custom-call | flops 134217728 | bytes 524288 | tf_op jit(solution)/shard_map/pallas_call | solution.py:229
  11.1 1.6 %collective-permute-done.1.refs_3_ = s32[16,1,128]{2,1,0:T(1,128)S(1)} collective-permute-done((s32[16,1,128]{2,1,0:T(1,128)S(1)}, s32[16,1,128]{2,1,0:T(1,128)S(1)}, u32[]{:S(2)}, u32[]{:S(2)}) %collective-permute-start.1) | collective-permute-done | bytes 8224 | tf_op jit(solution)/shard_map/ppermute | solution.py:183
  12.7 0.0 collective-permute-done.4.refs_6_
  12.7 0.6 %shard_map.60 = (bf16[9,128,128]{2,1,0:T(8,128)(2,1)S(1)}, f32[3,128,128]{2,1,0:T(8,128)S(1)}) custom-call(bf16[128,128]{1,0:T(8,128)(2,1)S(1)} %get-tuple-element.11.refs_0_, s32[16,1,128]{2,1,0:T(1,128)S(1)} %get-tuple-element.12.refs_1_, s32[16,1,128]{2,1,0:T(1,128)S(1)} %collective-permute-done.refs_2_, ...), custom_call_target="tpu_custom_call" | custom-call | flops 134217728 | bytes 524288 | tf_op jit(solution)/shard_map/pallas_call | solution.py:229
  13.3 0.0 collective-permute-done.2.refs_4_
  13.3 0.0 collective-permute-done.5.refs_8_
  13.3 1.1 %shard_map.61 = f32[32,1,256]{2,1,0:T(1,128)S(1)} custom-call(bf16[128,128]{1,0:T(8,128)(2,1)S(1)} %get-tuple-element.11.refs_0_, s32[16,1,128]{2,1,0:T(1,128)S(1)} %get-tuple-element.12.refs_1_, s32[16,1,128]{2,1,0:T(1,128)S(1)} %collective-permute-done.refs_2_, s32[16,1,128]{2,1,0:T(1,128)S(1)} %collective-permute-done.1.refs_3_, ...), custom_call_target="tpu_custom_call" | custom-call | flops 268435456 | bytes 524288 | tf_op jit(solution)/shard_map/pallas_call | solution.py:229
  14.4 11.9 %all_to_all.5.received = f32[32,1,256]{2,1,0:T(1,128)S(1)} all-to-all(f32[32,1,256]{2,1,0:T(1,128)S(1)} %shard_map.61), channel_id=1, replica_groups=mesh['grp'=8,'sub'=4] {'grp','sub'}, dimensions={0} | all-to-all | bytes 65536 | tf_op jit(solution)/shard_map/all_to_all | solution.py:233
  26.3 0.7 %last.1 = (f32[128]{0:T(128)}, f32[1]{0:T(128)}) custom-call(f32[32,1,256]{2,1,0:T(1,128)S(1)} %all_to_all.5.received), custom_call_target="tpu_custom_call" | custom-call | tf_op jit(solution)/shard_map/last/pallas_call | solution.py:234
Async XLA Ops:
  0.6 9.8 %collective-permute-start.3 = (bf16[8,128,128]{2,1,0:T(8,128)(2,1)}, bf16[8,128,128]{2,1,0:T(8,128)(2,1)S(1)}, u32[]{:S(2)}, u32[]{:S(2)}) collective-permute-start(bf16[8,128,128]{2,1,0:T(8,128)(2,1)} %raw.1), channel_id=1, source_target_pairs={{4,0},{0,4},{12,8},{8,12},{20,16},{16,20},{28,24},{24,28},{5,1},{1... | collective-permute-start | bytes 786440 | tf_op jit(solution)/shard_map/ppermute | solution.py:183
  1.2 11.5 %collective-permute-start.4 = (bf16[8,128,128]{2,1,0:T(8,128)(2,1)}, bf16[8,128,128]{2,1,0:T(8,128)(2,1)S(1)}, u32[]{:S(2)}, u32[]{:S(2)}) collective-permute-start(bf16[8,128,128]{2,1,0:T(8,128)(2,1)} %raw.1), channel_id=1, source_target_pairs={{8,0},{12,4},{0,8},{4,12},{24,16},{28,20},{16,24},{20,28},{9,1},{1... | collective-permute-start | bytes 786440 | tf_op jit(solution)/shard_map/ppermute | solution.py:183
  3.7 9.6 %collective-permute-start.5 = (bf16[8,128,128]{2,1,0:T(8,128)(2,1)}, bf16[8,128,128]{2,1,0:T(8,128)(2,1)S(1)}, u32[]{:S(2)}, u32[]{:S(2)}) collective-permute-start(bf16[8,128,128]{2,1,0:T(8,128)(2,1)} %raw.1), channel_id=1, source_target_pairs={{20,0},{16,4},{28,8},{24,12},{0,16},{4,20},{8,24},{12,28},{21,1},{... | collective-permute-start | bytes 786440 | tf_op jit(solution)/shard_map/ppermute | solution.py:183
  5.3 1.0 %copy-start = (bf16[8,128,128]{2,1,0:T(8,128)(2,1)S(1)}, bf16[8,128,128]{2,1,0:T(8,128)(2,1)}, u32[]{:S(2)}) copy-start(bf16[8,128,128]{2,1,0:T(8,128)(2,1)} %raw.1) | copy-start | bytes 786436
  6.2 0.7 %copy-start.1 = (s32[1,4,128]{2,1,0:T(4,128)S(1)}, s32[1,4,128]{2,1,0:T(4,128)}, u32[]{:S(2)}) copy-start(s32[1,4,128]{2,1,0:T(4,128)} %pair_lists.1) | copy-start | bytes 6148
  6.9 0.7 %copy-start.2 = (s32[1,32]{1,0:T(1,128)S(1)}, s32[1,32]{1,0:T(1,128)}, u32[]{:S(2)}) copy-start(s32[1,32]{1,0:T(1,128)} %far_slots.1) | copy-start | bytes 388
  7.6 0.7 %copy-start.3 = (s32[8]{0:T(128)S(1)}, s32[8]{0:T(128)}, u32[]{:S(2)}) copy-start(s32[8]{0:T(128)} %block_cols.1) | copy-start | bytes 100
  9.0 1.2 %collective-permute-start = (s32[16,1,128]{2,1,0:T(1,128)S(1)}, s32[16,1,128]{2,1,0:T(1,128)S(1)}, u32[]{:S(2)}, u32[]{:S(2)}) collective-permute-start(s32[16,1,128]{2,1,0:T(1,128)S(1)} %get-tuple-element.12.refs_1_), channel_id=1, source_target_pairs={{4,0},{0,4},{12,8},{8,12},{20,16},{16,20},{28,24},{24,28},{5,1},{1... | collective-permute-start | bytes 24584 | tf_op jit(solution)/shard_map/ppermute | solution.py:183
  9.0 3.7 %collective-permute-start.1 = (s32[16,1,128]{2,1,0:T(1,128)S(1)}, s32[16,1,128]{2,1,0:T(1,128)S(1)}, u32[]{:S(2)}, u32[]{:S(2)}) collective-permute-start(s32[16,1,128]{2,1,0:T(1,128)S(1)} %get-tuple-element.12.refs_1_), channel_id=1, source_target_pairs={{8,0},{12,4},{0,8},{4,12},{24,16},{28,20},{16,24},{20,28},{9,1},{1... | collective-permute-start | bytes 24584 | tf_op jit(solution)/shard_map/ppermute | solution.py:183
  10.2 3.2 %collective-permute-start.2 = (s32[16,1,128]{2,1,0:T(1,128)S(1)}, s32[16,1,128]{2,1,0:T(1,128)S(1)}, u32[]{:S(2)}, u32[]{:S(2)}) collective-permute-start(s32[16,1,128]{2,1,0:T(1,128)S(1)} %get-tuple-element.12.refs_1_), channel_id=1, source_target_pairs={{20,0},{16,4},{28,8},{24,12},{0,16},{4,20},{8,24},{12,28},{21,1},{... | collective-permute-start | bytes 24584 | tf_op jit(solution)/shard_map/ppermute | solution.py:183

commit v2 on v1

--- a/solution.py
+++ b/solution.py
@@ -12,6 +12,14 @@
 FIELD = 8
 
 
+def over(value, by):
+    return value >> (by.bit_length() - 1) if by & (by - 1) == 0 else value // by
+
+
+def rest(value, by):
+    return value & (by - 1) if by & (by - 1) == 0 else value % by
+
+
 class Places:
     def __init__(self, count):
         self.count = count
@@ -21,19 +29,19 @@
     def split(self, place):
         if self.cycle != 4:
             return (place, 0)
-        low = place % 2
-        high = place // (2 * self.mids)
+        low = rest(place, 2)
+        high = over(place, 2 * self.mids)
         turn = 2 * low + high * (3 - 4 * low)
-        return (turn, (place // 2) % self.mids)
+        return (turn, rest(over(place, 2), self.mids))
 
     def join(self, turn, mid):
         if self.cycle != 4:
             return turn
-        return (turn % 2) * 2 * self.mids + mid * 2 + ((turn + 1) // 2) % 2
+        return rest(turn, 2) * 2 * self.mids + mid * 2 + rest(over(turn + 1, 2), 2)
 
     def step(self, place, by):
         turn, mid = self.split(place)
-        return self.join((turn + by[0]) % self.cycle, (mid + by[1]) % self.mids)
+        return self.join(rest(turn + by[0], self.cycle), rest(mid + by[1], self.mids))
 
     def gap(self, there, here):
         return ((there[0] - here[0]) % self.cycle, (there[1] - here[1]) % self.mids)
@@ -67,17 +75,18 @@
         self.named = far_width // groups
         self.places = Places(groups)
         self.held, self.pairs = self.places.cover()
+        self.steps = list(itertools.product(range(self.places.cycle), range(self.places.mids)))
         self.near = 2 if (2, 0) in self.held and len(self.held) > 2 else 1
         self.order = sorted(range(len(self.held)), key=lambda i: (self.held[i] == (2, 0), i))
 
-    def group(self, i):
-        return self.places.step(lax.axis_index("grp"), self.held[i])
-
     def owner(self, i):
-        return self.group(i) * self.subs + lax.axis_index("sub")
-
-
-def pack_kernel(plan, pair_lists, far_slots, block_cols, raw, meta, strict, kept):
+        return self.places.step(lax.axis_index("grp"), self.held[i]) * self.subs + lax.axis_index("sub")
+
+    def at(self, i, j):
+        return self.steps.index(self.places.gap(self.held[j], self.held[i]))
+
+
+def pack_kernel(plan, pair_lists, far_slots, block_cols, raw, meta, strict, kept, by_group):
     groups, listed, named = plan.groups, plan.listed, plan.named
     stored, size = raw.shape[:2]
     left, place, mask, live = (pair_lists[0, field : field + 1] for field in range(4))
@@ -89,7 +98,9 @@
     far = jnp.dot(slots, wanted, preferred_element_type=jnp.float32)[:1].astype(jnp.int32)
     codes = left + far * 2**FIELD + jnp.where(live == 1, mask, stored) * 4**FIELD
     for group in range(groups):
-        meta[group, :, :listed] = codes[:, group * listed : (group + 1) * listed]
+        by_group[group, :, :listed] = codes[:, group * listed : (group + 1) * listed]
+    for at, step in enumerate(plan.steps):
+        meta[at] = by_group[plan.places.step(lax.axis_index("grp"), step)]
     for slot in range(stored):
         meta[groups + slot] = jnp.full((1, size), block_cols[slot] != plan.owner(0), meta.dtype)
     rows = lax.broadcasted_iota(jnp.int32, (size, size), 0)
@@ -143,7 +154,7 @@
         acc = before[i] if i < done else jnp.zeros((size, size), jnp.float32)
         for row, j in pairs:
             if row == i:
-                acc = add_triples(plan, acc, kept[i], kept[i], kept[j], metas[i][plan.group(j)])
+                acc = add_triples(plan, acc, kept[i], kept[i], kept[j], metas[i][plan.at(i, j)])
         if last:
             sums[i] = jnp.sum(acc.T, axis=0, keepdims=True)
         else:
@@ -196,9 +207,10 @@
         ],
         in_specs=[vmem, vmem, smem, vmem],
         out_specs=[vmem, vmem, vmem],
+        scratch_shapes=[pltpu.VMEM((groups, 1, size), jnp.int32)],
         compiler_params=own_vmem,
         name="pack",
-    )(pair_lists, far_slots, block_cols, blocks)
+    )(*(pltpu.with_memory_space_constraint(a, pltpu.HBM) for a in (pair_lists, far_slots, block_cols, blocks)))
     metas = {i: brought(meta, i) for i in plan.order}
 
     stages = [range(1, plan.near)] + [range(i, i + 1) for i in range(plan.near, len(held))]

time: 27.2 us -> 26.7 us (0.982)
  local copies, waits for them, and re-layouts: 2.97 us -> 0 us
  waiting for transfers between devices: 2.2 us -> 3.72 us
  blocking collectives: 11.9 us -> 12.4 us
  Pallas kernels: 3.72 us -> 4.14 us
    unnamed x8 -> x0, local copies, waits for them, and re-layouts: 2.97 us -> none
    ppermute x6, waiting for transfers between devices: 2.2 us -> 3.72 us  [brought(): return lax.ppermute(array, 'grp', pairs)]
    all_to_all x1, blocking collectives: 11.9 us -> 12.4 us  [local(): lax.all_to_all(out, ('grp', 'sub'), split_axis=0, concat_axis=0, tiled=True)]
    pallas_call x1, Pallas kernels: 0.74 us -> 1.27 us  [local(): pl.pallas_call(functools.partial(pack_kernel, plan), out_shape=[pltpu.VME...]
  transfers between devices with their start and end apart: 6 -> 6, of which waited for: 2 -> 3; matrix products, arithmetic and copies ran while one was open for 0% -> 0% of each run, Pallas kernels for 7% -> 9%
where the time goes in v2:
time: 26.7 us; the launch traced here: 26.5 us
  blocking collectives  12.4 us (46%)
  starting transfers between devices  5.58 us (21%)
  Pallas kernels  4.14 us (16%)
  waiting for transfers between devices  3.72 us (14%)
  between operations  0.66 us (2%)
    all_to_all x1, blocking collectives, local(): lax.all_to_all(out, ('grp', 'sub'), split_axis=0, concat_axis=0, tiled=True)  12.4 us
    ppermute x6, starting transfers between devices, brought(): return lax.ppermute(array, 'grp', pairs)  5.58 us
    ppermute x6, waiting for transfers between devices, brought(): return lax.ppermute(array, 'grp', pairs)  3.72 us
    pallas_call x3, Pallas kernels, local(): out = call(*operands)  2.21 us
    pallas_call x1, Pallas kernels, local(): pl.pallas_call(functools.partial(pack_kernel, plan), out_shape=[pltpu.VME...  1.27 us
    pallas_call x1, Pallas kernels, local(): pl.pallas_call(functools.partial(last_kernel, math.sqrt(groups * subs * s...  0.66 us
  transfers between devices with their start and end apart: 6, of which 3 were waited for; matrix products, arithmetic and copies ran while one was open for 0% of the time, Pallas kernels for 9%

profile of v2, /device:TPU:0, one launch (start us, length us, event | category | flops | bytes accessed | tf_op | source)
XLA Modules:
  0.0 26.5 jit_solution(14503446393420056822)
XLA Ops:
  0.6 0.6 %collective-permute-start.3 = (bf16[8,128,128]{2,1,0:T(8,128)(2,1)}, bf16[8,128,128]{2,1,0:T(8,128)(2,1)S(1)}, u32[]{:S(2)}, u32[]{:S(2)}) collective-permute-start(bf16[8,128,128]{2,1,0:T(8,128)(2,1)} %raw.1), channel_id=1, source_target_pairs={{4,0},{0,4},{12,8},{8,12},{20,16},{16,20},{28,24},{24,28},{5,1},{1... | collective-permute-start | bytes 786440 | tf_op jit(solution)/shard_map/ppermute | solution.py:194
  1.2 2.6 %collective-permute-start.4 = (bf16[8,128,128]{2,1,0:T(8,128)(2,1)}, bf16[8,128,128]{2,1,0:T(8,128)(2,1)S(1)}, u32[]{:S(2)}, u32[]{:S(2)}) collective-permute-start(bf16[8,128,128]{2,1,0:T(8,128)(2,1)} %raw.1), channel_id=1, source_target_pairs={{8,0},{12,4},{0,8},{4,12},{24,16},{28,20},{16,24},{20,28},{9,1},{1... | collective-permute-start | bytes 786440 | tf_op jit(solution)/shard_map/ppermute | solution.py:194
  3.7 1.5 %collective-permute-start.5 = (bf16[8,128,128]{2,1,0:T(8,128)(2,1)}, bf16[8,128,128]{2,1,0:T(8,128)(2,1)S(1)}, u32[]{:S(2)}, u32[]{:S(2)}) collective-permute-start(bf16[8,128,128]{2,1,0:T(8,128)(2,1)} %raw.1), channel_id=1, source_target_pairs={{20,0},{16,4},{28,8},{24,12},{0,16},{4,20},{8,24},{12,28},{21,1},{... | collective-permute-start | bytes 786440 | tf_op jit(solution)/shard_map/ppermute | solution.py:194
  5.3 1.3 %pack.1 = (s32[16,1,128]{2,1,0:T(1,128)S(1)}, bf16[128,128]{1,0:T(8,128)(2,1)S(1)}, bf16[9,128,128]{2,1,0:T(8,128)(2,1)S(1)}) custom-call(s32[1,4,128]{2,1,0:T(4,128)} %pair_lists.1, s32[1,32]{1,0:T(1,128)} %far_slots.1, s32[8]{0:T(128)} %block_cols.1, bf16[8,128,128]{2,1,0:T(8,128)(2,1)} %raw.1), custom_call_target="tpu_custom_call" | custom-call | tf_op jit(solution)/shard_map/pack/pallas_call | solution.py:201
  6.5 0.1 collective-permute-start
  6.6 0.6 %collective-permute-start.1 = (s32[16,1,128]{2,1,0:T(1,128)S(1)}, s32[16,1,128]{2,1,0:T(1,128)S(1)}, u32[]{:S(2)}, u32[]{:S(2)}) collective-permute-start(s32[16,1,128]{2,1,0:T(1,128)S(1)} %get-tuple-element.12.refs_1_), channel_id=1, source_target_pairs={{8,0},{12,4},{0,8},{4,12},{24,16},{28,20},{16,24},{20,28},{9,1},{1... | collective-permute-start | bytes 24584 | tf_op jit(solution)/shard_map/ppermute | solution.py:194
  7.2 0.6 %collective-permute-done.refs_2_ = s32[16,1,128]{2,1,0:T(1,128)S(1)} collective-permute-done((s32[16,1,128]{2,1,0:T(1,128)S(1)}, s32[16,1,128]{2,1,0:T(1,128)S(1)}, u32[]{:S(2)}, u32[]{:S(2)}) %collective-permute-start) | collective-permute-done | bytes 8224 | tf_op jit(solution)/shard_map/ppermute | solution.py:194
  7.8 0.3 %collective-permute-start.2 = (s32[16,1,128]{2,1,0:T(1,128)S(1)}, s32[16,1,128]{2,1,0:T(1,128)S(1)}, u32[]{:S(2)}, u32[]{:S(2)}) collective-permute-start(s32[16,1,128]{2,1,0:T(1,128)S(1)} %get-tuple-element.12.refs_1_), channel_id=1, source_target_pairs={{20,0},{16,4},{28,8},{24,12},{0,16},{4,20},{8,24},{12,28},{21,1},{... | collective-permute-start | bytes 24584 | tf_op jit(solution)/shard_map/ppermute | solution.py:194
  8.0 0.0 collective-permute-done.3.refs_4_
  8.1 0.6 %shard_map.59 = (bf16[9,128,128]{2,1,0:T(8,128)(2,1)S(1)}, f32[2,128,128]{2,1,0:T(8,128)S(1)}) custom-call(bf16[128,128]{1,0:T(8,128)(2,1)S(1)} %get-tuple-element.11.refs_0_, s32[16,1,128]{2,1,0:T(1,128)S(1)} %get-tuple-element.12.refs_1_, s32[16,1,128]{2,1,0:T(1,128)S(1)} %collective-permute-done.refs_2_, ...), custom_call_target="tpu_custom_call" | custom-call | flops 134217728 | bytes 524288 | tf_op jit(solution)/shard_map/pallas_call | solution.py:241
  8.7 2.3 %collective-permute-done.1.refs_3_ = s32[16,1,128]{2,1,0:T(1,128)S(1)} collective-permute-done((s32[16,1,128]{2,1,0:T(1,128)S(1)}, s32[16,1,128]{2,1,0:T(1,128)S(1)}, u32[]{:S(2)}, u32[]{:S(2)}) %collective-permute-start.1) | collective-permute-done | bytes 8224 | tf_op jit(solution)/shard_map/ppermute | solution.py:194
  11.0 0.0 collective-permute-done.4.refs_6_
  11.0 0.5 %shard_map.60 = (bf16[9,128,128]{2,1,0:T(8,128)(2,1)S(1)}, f32[3,128,128]{2,1,0:T(8,128)S(1)}) custom-call(bf16[128,128]{1,0:T(8,128)(2,1)S(1)} %get-tuple-element.11.refs_0_, s32[16,1,128]{2,1,0:T(1,128)S(1)} %get-tuple-element.12.refs_1_, s32[16,1,128]{2,1,0:T(1,128)S(1)} %collective-permute-done.refs_2_, ...), custom_call_target="tpu_custom_call" | custom-call | flops 134217728 | bytes 524288 | tf_op jit(solution)/shard_map/pallas_call | solution.py:241
  11.6 0.8 %collective-permute-done.2.refs_4_ = s32[16,1,128]{2,1,0:T(1,128)S(1)} collective-permute-done((s32[16,1,128]{2,1,0:T(1,128)S(1)}, s32[16,1,128]{2,1,0:T(1,128)S(1)}, u32[]{:S(2)}, u32[]{:S(2)}) %collective-permute-start.2) | collective-permute-done | bytes 8224 | tf_op jit(solution)/shard_map/ppermute | solution.py:194
  12.4 0.0 collective-permute-done.5.refs_8_
  12.4 1.0 %shard_map.61 = f32[32,1,256]{2,1,0:T(1,128)S(1)} custom-call(bf16[128,128]{1,0:T(8,128)(2,1)S(1)} %get-tuple-element.11.refs_0_, s32[16,1,128]{2,1,0:T(1,128)S(1)} %get-tuple-element.12.refs_1_, s32[16,1,128]{2,1,0:T(1,128)S(1)} %collective-permute-done.refs_2_, s32[16,1,128]{2,1,0:T(1,128)S(1)} %collective-permute-done.1.refs_3_, ...), custom_call_target="tpu_custom_call" | custom-call | flops 268435456 | bytes 524288 | tf_op jit(solution)/shard_map/pallas_call | solution.py:241
  13.4 12.4 %all_to_all.5.received = f32[32,1,256]{2,1,0:T(1,128)S(1)} all-to-all(f32[32,1,256]{2,1,0:T(1,128)S(1)} %shard_map.61), channel_id=1, replica_groups=mesh['grp'=8,'sub'=4] {'grp','sub'}, dimensions={0} | all-to-all | bytes 65536 | tf_op jit(solution)/shard_map/all_to_all | solution.py:245
  25.9 0.7 %last.1 = (f32[128]{0:T(128)}, f32[1]{0:T(128)}) custom-call(f32[32,1,256]{2,1,0:T(1,128)S(1)} %all_to_all.5.received), custom_call_target="tpu_custom_call" | custom-call | tf_op jit(solution)/shard_map/last/pallas_call | solution.py:246
Async XLA Ops:
  0.6 7.4 %collective-permute-start.3 = (bf16[8,128,128]{2,1,0:T(8,128)(2,1)}, bf16[8,128,128]{2,1,0:T(8,128)(2,1)S(1)}, u32[]{:S(2)}, u32[]{:S(2)}) collective-permute-start(bf16[8,128,128]{2,1,0:T(8,128)(2,1)} %raw.1), channel_id=1, source_target_pairs={{4,0},{0,4},{12,8},{8,12},{20,16},{16,20},{28,24},{24,28},{5,1},{1... | collective-permute-start | bytes 786440 | tf_op jit(solution)/shard_map/ppermute | solution.py:194
  1.2 9.8 %collective-permute-start.4 = (bf16[8,128,128]{2,1,0:T(8,128)(2,1)}, bf16[8,128,128]{2,1,0:T(8,128)(2,1)S(1)}, u32[]{:S(2)}, u32[]{:S(2)}) collective-permute-start(bf16[8,128,128]{2,1,0:T(8,128)(2,1)} %raw.1), channel_id=1, source_target_pairs={{8,0},{12,4},{0,8},{4,12},{24,16},{28,20},{16,24},{20,28},{9,1},{1... | collective-permute-start | bytes 786440 | tf_op jit(solution)/shard_map/ppermute | solution.py:194
  3.7 8.7 %collective-permute-start.5 = (bf16[8,128,128]{2,1,0:T(8,128)(2,1)}, bf16[8,128,128]{2,1,0:T(8,128)(2,1)S(1)}, u32[]{:S(2)}, u32[]{:S(2)}) collective-permute-start(bf16[8,128,128]{2,1,0:T(8,128)(2,1)} %raw.1), channel_id=1, source_target_pairs={{20,0},{16,4},{28,8},{24,12},{0,16},{4,20},{8,24},{12,28},{21,1},{... | collective-permute-start | bytes 786440 | tf_op jit(solution)/shard_map/ppermute | solution.py:194
  6.5 1.2 %collective-permute-start = (s32[16,1,128]{2,1,0:T(1,128)S(1)}, s32[16,1,128]{2,1,0:T(1,128)S(1)}, u32[]{:S(2)}, u32[]{:S(2)}) collective-permute-start(s32[16,1,128]{2,1,0:T(1,128)S(1)} %get-tuple-element.12.refs_1_), channel_id=1, source_target_pairs={{4,0},{0,4},{12,8},{8,12},{20,16},{16,20},{28,24},{24,28},{5,1},{1... | collective-permute-start | bytes 24584 | tf_op jit(solution)/shard_map/ppermute | solution.py:194
  6.6 4.4 %collective-permute-start.1 = (s32[16,1,128]{2,1,0:T(1,128)S(1)}, s32[16,1,128]{2,1,0:T(1,128)S(1)}, u32[]{:S(2)}, u32[]{:S(2)}) collective-permute-start(s32[16,1,128]{2,1,0:T(1,128)S(1)} %get-tuple-element.12.refs_1_), channel_id=1, source_target_pairs={{8,0},{12,4},{0,8},{4,12},{24,16},{28,20},{16,24},{20,28},{9,1},{1... | collective-permute-start | bytes 24584 | tf_op jit(solution)/shard_map/ppermute | solution.py:194
  7.8 4.6 %collective-permute-start.2 = (s32[16,1,128]{2,1,0:T(1,128)S(1)}, s32[16,1,128]{2,1,0:T(1,128)S(1)}, u32[]{:S(2)}, u32[]{:S(2)}) collective-permute-start(s32[16,1,128]{2,1,0:T(1,128)S(1)} %get-tuple-element.12.refs_1_), channel_id=1, source_target_pairs={{20,0},{16,4},{28,8},{24,12},{0,16},{4,20},{8,24},{12,28},{21,1},{... | collective-permute-start | bytes 24584 | tf_op jit(solution)/shard_map/ppermute | solution.py:194

commit v3 on v2

--- a/solution.py
+++ b/solution.py
@@ -9,56 +9,47 @@
 from jax.experimental.pallas import tpu as pltpu
 from jax.sharding import PartitionSpec as P
 
+FIRST = -1
 FIELD = 8
-
-
-def over(value, by):
-    return value >> (by.bit_length() - 1) if by & (by - 1) == 0 else value // by
-
-
-def rest(value, by):
-    return value & (by - 1) if by & (by - 1) == 0 else value % by
 
 
 class Places:
     def __init__(self, count):
         self.count = count
-        self.cycle = 4 if count % 4 == 0 else count
-        self.mids = count // self.cycle
+        self.chips = count // 2
+        self.paired = count % 2 == 0 and self.chips & (self.chips - 1) == 0
 
     def split(self, place):
-        if self.cycle != 4:
-            return (place, 0)
-        low = rest(place, 2)
-        high = over(place, 2 * self.mids)
-        turn = 2 * low + high * (3 - 4 * low)
-        return (turn, rest(over(place, 2), self.mids))
-
-    def join(self, turn, mid):
-        if self.cycle != 4:
-            return turn
-        return rest(turn, 2) * 2 * self.mids + mid * 2 + rest(over(turn + 1, 2), 2)
+        if not self.paired:
+            return place
+        turn = place >> 1
+        shift = 1
+        while shift < self.chips:
+            turn = turn ^ (turn >> shift)
+            shift *= 2
+        return turn + (place & 1) * self.chips
 
     def step(self, place, by):
-        turn, mid = self.split(place)
-        return self.join(rest(turn + by[0], self.cycle), rest(mid + by[1], self.mids))
+        turn = self.split(place) + by
+        if not self.paired:
+            return turn % self.count
+        turn = turn & (self.count - 1)
+        chip = turn & (self.chips - 1)
+        return (chip ^ (chip >> 1)) * 2 + (turn >> (self.chips.bit_length() - 1))
 
     def gap(self, there, here):
-        return ((there[0] - here[0]) % self.cycle, (there[1] - here[1]) % self.mids)
+        return (there - here) % self.count
 
     def cover(self):
-        steps = sorted(
-            itertools.product(range(self.cycle), range(self.mids)),
-            key=lambda s: ((s[0] > 0) + (s[1] > 0), s),
-        )
-
         def reached(chosen):
             return {self.gap(a, b) for a in chosen for b in chosen}
 
-        chosen = [(0, 0)]
-        while len(reached(chosen)) < self.count:
-            chosen.append(max(steps, key=lambda s: len(reached(chosen + [s]))))
-        held = sorted(chosen, key=lambda s: (s != (0, 0), s != (2, 0), s))
+        held = [0]
+        for step in (self.chips, FIRST % self.count, -FIRST % self.count):
+            if step not in held and len(reached(held)) < self.count:
+                held.append(step)
+        while len(reached(held)) < self.count:
+            held.append(max(range(self.count), key=lambda s: len(reached(held + [s]))))
         pairs = {}
         for (i, row), (j, source) in itertools.product(enumerate(held), enumerate(held)):
             wanted = self.gap(source, row)
@@ -75,15 +66,14 @@
         self.named = far_width // groups
         self.places = Places(groups)
         self.held, self.pairs = self.places.cover()
-        self.steps = list(itertools.product(range(self.places.cycle), range(self.places.mids)))
-        self.near = 2 if (2, 0) in self.held and len(self.held) > 2 else 1
-        self.order = sorted(range(len(self.held)), key=lambda i: (self.held[i] == (2, 0), i))
+        self.near = min(2, len(self.held) - 1)
+        self.order = [0] + list(range(self.near, len(self.held))) + list(range(1, self.near))
 
     def owner(self, i):
         return self.places.step(lax.axis_index("grp"), self.held[i]) * self.subs + lax.axis_index("sub")
 
     def at(self, i, j):
-        return self.steps.index(self.places.gap(self.held[j], self.held[i]))
+        return self.places.gap(self.held[j], self.held[i])
 
 
 def pack_kernel(plan, pair_lists, far_slots, block_cols, raw, meta, strict, kept, by_group):
@@ -99,8 +89,8 @@
     codes = left + far * 2**FIELD + jnp.where(live == 1, mask, stored) * 4**FIELD
     for group in range(groups):
         by_group[group, :, :listed] = codes[:, group * listed : (group + 1) * listed]
-    for at, step in enumerate(plan.steps):
-        meta[at] = by_group[plan.places.step(lax.axis_index("grp"), step)]
+    for step in range(groups):
+        meta[step] = by_group[plan.places.step(lax.axis_index("grp"), step)]
     for slot in range(stored):
         meta[groups + slot] = jnp.full((1, size), block_cols[slot] != plan.owner(0), meta.dtype)
     rows = lax.broadcasted_iota(jnp.int32, (size, size), 0)
@@ -171,7 +161,7 @@
     size = participation.shape[0]
     summed = jnp.sum(received[:, 0, :], axis=0, keepdims=True)
     participation[...] = summed[0, :size]
-    total[0] = jnp.sum(summed[:, size:]) / divisor
+    total[...] = (jnp.sum(summed[:, size:], axis=1, keepdims=True) / divisor)[0]
 
 
 def in_vmem(array):
@@ -247,7 +237,7 @@
         functools.partial(last_kernel, math.sqrt(groups * subs * size)),
         out_shape=[jax.ShapeDtypeStruct((size,), jnp.float32), jax.ShapeDtypeStruct((1,), jnp.float32)],
         in_specs=[vmem],
-        out_specs=[vmem, smem],
+        out_specs=[vmem, vmem],
         compiler_params=own_vmem,
         name="last",
     )(received)

time: 26.7 us -> 26.6 us (level)
  waiting for transfers between devices: 3.72 us -> 2.91 us
  starting transfers between devices: 5.58 us -> 6.16 us
    ppermute x6, waiting for transfers between devices: 3.72 us -> 2.91 us  [brought(): return lax.ppermute(array, 'grp', pairs)]
    ppermute x6, starting transfers between devices: 5.58 us -> 6.16 us  [brought(): return lax.ppermute(array, 'grp', pairs)]
  transfers between devices with their start and end apart: 6 -> 6, of which waited for: 3 -> 2; matrix products, arithmetic and copies ran while one was open for 0% -> 0% of each run, Pallas kernels for 9% -> 10%
where the time goes in v3:
time: 26.6 us; the launch traced here: 26.4 us
  blocking collectives  12.6 us (47%)
  starting transfers between devices  6.16 us (23%)
  Pallas kernels  4.05 us (15%)
  waiting for transfers between devices  2.91 us (11%)
  between operations  0.66 us (2%)
    all_to_all x1, blocking collectives, local(): lax.all_to_all(out, ('grp', 'sub'), split_axis=0, concat_axis=0, tiled=True)  12.6 us
    ppermute x6, starting transfers between devices, brought(): return lax.ppermute(array, 'grp', pairs)  6.16 us
    ppermute x6, waiting for transfers between devices, brought(): return lax.ppermute(array, 'grp', pairs)  2.91 us
    pallas_call x3, Pallas kernels, local(): out = call(*operands)  2.17 us
    pallas_call x1, Pallas kernels, local(): pl.pallas_call(functools.partial(pack_kernel, plan), out_shape=[pltpu.VME...  1.27 us
    pallas_call x1, Pallas kernels, local(): pl.pallas_call(functools.partial(last_kernel, math.sqrt(groups * subs * s...  0.61 us
  transfers between devices with their start and end apart: 6, of which 2 were waited for; matrix products, arithmetic and copies ran while one was open for 0% of the time, Pallas kernels for 10%

profile of v3, /device:TPU:0, one launch (start us, length us, event | category | flops | bytes accessed | tf_op | source)
XLA Modules:
  0.0 26.4 jit_solution(10126356309627976370)
XLA Ops:
  0.6 0.6 %collective-permute-start.3 = (bf16[8,128,128]{2,1,0:T(8,128)(2,1)}, bf16[8,128,128]{2,1,0:T(8,128)(2,1)S(1)}, u32[]{:S(2)}, u32[]{:S(2)}) collective-permute-start(bf16[8,128,128]{2,1,0:T(8,128)(2,1)} %raw.1), channel_id=1, source_target_pairs={{4,0},{0,4},{12,8},{8,12},{20,16},{16,20},{28,24},{24,28},{5,1},{1... | collective-permute-start | bytes 786440 | tf_op jit(solution)/shard_map/ppermute | solution.py:184
  1.2 2.5 %collective-permute-start.4 = (bf16[8,128,128]{2,1,0:T(8,128)(2,1)}, bf16[8,128,128]{2,1,0:T(8,128)(2,1)S(1)}, u32[]{:S(2)}, u32[]{:S(2)}) collective-permute-start(bf16[8,128,128]{2,1,0:T(8,128)(2,1)} %raw.1), channel_id=1, source_target_pairs={{20,0},{16,4},{0,8},{4,12},{24,16},{28,20},{8,24},{12,28},{21,1},{... | collective-permute-start | bytes 786440 | tf_op jit(solution)/shard_map/ppermute | solution.py:184
  3.7 0.1 collective-permute-start.5
  3.8 1.3 %pack.1 = (s32[16,1,128]{2,1,0:T(1,128)S(1)}, bf16[128,128]{1,0:T(8,128)(2,1)S(1)}, bf16[9,128,128]{2,1,0:T(8,128)(2,1)S(1)}) custom-call(s32[1,4,128]{2,1,0:T(4,128)} %pair_lists.1, s32[1,32]{1,0:T(1,128)} %far_slots.1, s32[8]{0:T(128)} %block_cols.1, bf16[8,128,128]{2,1,0:T(8,128)(2,1)} %raw.1), custom_call_target="tpu_custom_call" | custom-call | tf_op jit(solution)/shard_map/pack/pallas_call | solution.py:191
  5.1 0.2 collective-permute-start
  5.3 1.9 %collective-permute-start.1 = (s32[16,1,128]{2,1,0:T(1,128)S(1)}, s32[16,1,128]{2,1,0:T(1,128)S(1)}, u32[]{:S(2)}, u32[]{:S(2)}) collective-permute-start(s32[16,1,128]{2,1,0:T(1,128)S(1)} %get-tuple-element.12.refs_1_), channel_id=1, source_target_pairs={{20,0},{16,4},{0,8},{4,12},{24,16},{28,20},{8,24},{12,28},{21,1},{... | collective-permute-start | bytes 24584 | tf_op jit(solution)/shard_map/ppermute | solution.py:184
  7.2 0.0 collective-permute-done.refs_2_
  7.2 0.9 %collective-permute-start.2 = (s32[16,1,128]{2,1,0:T(1,128)S(1)}, s32[16,1,128]{2,1,0:T(1,128)S(1)}, u32[]{:S(2)}, u32[]{:S(2)}) collective-permute-start(s32[16,1,128]{2,1,0:T(1,128)S(1)} %get-tuple-element.12.refs_1_), channel_id=1, source_target_pairs={{8,0},{12,4},{24,8},{28,12},{4,16},{0,20},{16,24},{20,28},{9,1},{1... | collective-permute-start | bytes 24584 | tf_op jit(solution)/shard_map/ppermute | solution.py:184
  8.1 0.0 collective-permute-done.3.refs_4_
  8.1 0.6 %shard_map.59 = (bf16[9,128,128]{2,1,0:T(8,128)(2,1)S(1)}, f32[2,128,128]{2,1,0:T(8,128)S(1)}) custom-call(bf16[128,128]{1,0:T(8,128)(2,1)S(1)} %get-tuple-element.11.refs_0_, s32[16,1,128]{2,1,0:T(1,128)S(1)} %get-tuple-element.12.refs_1_, s32[16,1,128]{2,1,0:T(1,128)S(1)} %collective-permute-done.refs_2_, ...), custom_call_target="tpu_custom_call" | custom-call | flops 134217728 | bytes 524288 | tf_op jit(solution)/shard_map/pallas_call | solution.py:231
  8.7 2.1 %collective-permute-done.1.refs_3_ = s32[16,1,128]{2,1,0:T(1,128)S(1)} collective-permute-done((s32[16,1,128]{2,1,0:T(1,128)S(1)}, s32[16,1,128]{2,1,0:T(1,128)S(1)}, u32[]{:S(2)}, u32[]{:S(2)}) %collective-permute-start.1) | collective-permute-done | bytes 8224 | tf_op jit(solution)/shard_map/ppermute | solution.py:184
  10.8 0.0 collective-permute-done.4.refs_6_
  10.8 0.9 %shard_map.60 = (bf16[9,128,128]{2,1,0:T(8,128)(2,1)S(1)}, f32[3,128,128]{2,1,0:T(8,128)S(1)}) custom-call(bf16[128,128]{1,0:T(8,128)(2,1)S(1)} %get-tuple-element.11.refs_0_, s32[16,1,128]{2,1,0:T(1,128)S(1)} %get-tuple-element.12.refs_1_, s32[16,1,128]{2,1,0:T(1,128)S(1)} %collective-permute-done.refs_2_, ...), custom_call_target="tpu_custom_call" | custom-call | flops 268435456 | bytes 524288 | tf_op jit(solution)/shard_map/pallas_call | solution.py:231
  11.7 0.8 %collective-permute-done.2.refs_4_ = s32[16,1,128]{2,1,0:T(1,128)S(1)} collective-permute-done((s32[16,1,128]{2,1,0:T(1,128)S(1)}, s32[16,1,128]{2,1,0:T(1,128)S(1)}, u32[]{:S(2)}, u32[]{:S(2)}) %collective-permute-start.2) | collective-permute-done | bytes 8224 | tf_op jit(solution)/shard_map/ppermute | solution.py:184
  12.5 0.0 collective-permute-done.5.refs_8_
  12.5 0.7 %shard_map.61 = f32[32,1,256]{2,1,0:T(1,128)S(1)} custom-call(bf16[128,128]{1,0:T(8,128)(2,1)S(1)} %get-tuple-element.11.refs_0_, s32[16,1,128]{2,1,0:T(1,128)S(1)} %get-tuple-element.12.refs_1_, s32[16,1,128]{2,1,0:T(1,128)S(1)} %collective-permute-done.refs_2_, s32[16,1,128]{2,1,0:T(1,128)S(1)} %collective-permute-done.1.refs_3_, ...), custom_call_target="tpu_custom_call" | custom-call | flops 134217728 | bytes 524288 | tf_op jit(solution)/shard_map/pallas_call | solution.py:231
  13.2 12.6 %all_to_all.5.received = f32[32,1,256]{2,1,0:T(1,128)S(1)} all-to-all(f32[32,1,256]{2,1,0:T(1,128)S(1)} %shard_map.61), channel_id=1, replica_groups=mesh['grp'=8,'sub'=4] {'grp','sub'}, dimensions={0} | all-to-all | bytes 65536 | tf_op jit(solution)/shard_map/all_to_all | solution.py:235
  25.8 0.6 %last.1 = (f32[128]{0:T(128)}, f32[1]{0:T(128)}) custom-call(f32[32,1,256]{2,1,0:T(1,128)S(1)} %all_to_all.5.received), custom_call_target="tpu_custom_call" | custom-call | tf_op jit(solution)/shard_map/last/pallas_call | solution.py:236
Async XLA Ops:
  0.6 7.4 %collective-permute-start.3 = (bf16[8,128,128]{2,1,0:T(8,128)(2,1)}, bf16[8,128,128]{2,1,0:T(8,128)(2,1)S(1)}, u32[]{:S(2)}, u32[]{:S(2)}) collective-permute-start(bf16[8,128,128]{2,1,0:T(8,128)(2,1)} %raw.1), channel_id=1, source_target_pairs={{4,0},{0,4},{12,8},{8,12},{20,16},{16,20},{28,24},{24,28},{5,1},{1... | collective-permute-start | bytes 786440 | tf_op jit(solution)/shard_map/ppermute | solution.py:184
  1.2 9.6 %collective-permute-start.4 = (bf16[8,128,128]{2,1,0:T(8,128)(2,1)}, bf16[8,128,128]{2,1,0:T(8,128)(2,1)S(1)}, u32[]{:S(2)}, u32[]{:S(2)}) collective-permute-start(bf16[8,128,128]{2,1,0:T(8,128)(2,1)} %raw.1), channel_id=1, source_target_pairs={{20,0},{16,4},{0,8},{4,12},{24,16},{28,20},{8,24},{12,28},{21,1},{... | collective-permute-start | bytes 786440 | tf_op jit(solution)/shard_map/ppermute | solution.py:184
  3.7 8.8 %collective-permute-start.5 = (bf16[8,128,128]{2,1,0:T(8,128)(2,1)}, bf16[8,128,128]{2,1,0:T(8,128)(2,1)S(1)}, u32[]{:S(2)}, u32[]{:S(2)}) collective-permute-start(bf16[8,128,128]{2,1,0:T(8,128)(2,1)} %raw.1), channel_id=1, source_target_pairs={{8,0},{12,4},{24,8},{28,12},{4,16},{0,20},{16,24},{20,28},{9,1},{1... | collective-permute-start | bytes 786440 | tf_op jit(solution)/shard_map/ppermute | solution.py:184
  5.1 2.1 %collective-permute-start = (s32[16,1,128]{2,1,0:T(1,128)S(1)}, s32[16,1,128]{2,1,0:T(1,128)S(1)}, u32[]{:S(2)}, u32[]{:S(2)}) collective-permute-start(s32[16,1,128]{2,1,0:T(1,128)S(1)} %get-tuple-element.12.refs_1_), channel_id=1, source_target_pairs={{4,0},{0,4},{12,8},{8,12},{20,16},{16,20},{28,24},{24,28},{5,1},{1... | collective-permute-start | bytes 24584 | tf_op jit(solution)/shard_map/ppermute | solution.py:184
  5.3 5.5 %collective-permute-start.1 = (s32[16,1,128]{2,1,0:T(1,128)S(1)}, s32[16,1,128]{2,1,0:T(1,128)S(1)}, u32[]{:S(2)}, u32[]{:S(2)}) collective-permute-start(s32[16,1,128]{2,1,0:T(1,128)S(1)} %get-tuple-element.12.refs_1_), channel_id=1, source_target_pairs={{20,0},{16,4},{0,8},{4,12},{24,16},{28,20},{8,24},{12,28},{21,1},{... | collective-permute-start | bytes 24584 | tf_op jit(solution)/shard_map/ppermute | solution.py:184
  7.2 5.3 %collective-permute-start.2 = (s32[16,1,128]{2,1,0:T(1,128)S(1)}, s32[16,1,128]{2,1,0:T(1,128)S(1)}, u32[]{:S(2)}, u32[]{:S(2)}) collective-permute-start(s32[16,1,128]{2,1,0:T(1,128)S(1)} %get-tuple-element.12.refs_1_), channel_id=1, source_target_pairs={{8,0},{12,4},{24,8},{28,12},{4,16},{0,20},{16,24},{20,28},{9,1},{1... | collective-permute-start | bytes 24584 | tf_op jit(solution)/shard_map/ppermute | solution.py:184
